TPU v7x, 32 devices: a whole 2x2x4 slice. The times are simulated.
32 devices in a mesh: req: 8 (over z, y), tp: 4 (over x, core).
Axes of the slice: x: 2, y: 2, z: 4, core: 2. Of those that a mesh axis runs over, the one named last changes fastest.
Arguments:
- hidden_in: bfloat16 [512, 2048], P('req'), may hold values from -6 to 6
- queries: bfloat16 [512, 2048], P('req', 'tp'), may hold values from -200 to 200, as said below
- keys_new: bfloat16 [512, 2048], P('req', 'tp'), may hold values from -6 to 6
- values_new: bfloat16 [512, 2048], P('req', 'tp'), may hold values from -6 to 6
- prefix_keys: bfloat16 [8, 16, 2048], P('req', None, 'tp'), may hold values from -6 to 6
- prefix_values: bfloat16 [8, 16, 2048], P('req', None, 'tp'), may hold values from -6 to 6
- block_group: int32 [8], P('req'), may hold values from 0 to 1, as said below
- req_group: int32 [8], P('req'), may hold values from 0 to 1
- lengths: int32 [8], P('req'), may hold values from 1 to 64, 320 in all
- w_out: bfloat16 [2048, 2048], P('tp'), may hold values from -0.125 to 0.125
- norm_gain: bfloat16 [2048], replicated, may hold values from 0.25 to 1.75
- w_router: float32 [2048, 64], replicated, may hold values from -7 to 7
- routes: int32 [512, 8], P('req'), may hold values from 0 to 63, all different within a row; in each aligned block of 64 rows (0 to 63, 64 to 127, ...) at most 10 rows name the same one
- w_gate: bfloat16 [128, 2048, 512], P('req', None, 'tp'), may hold values from -0.125 to 0.125
- w_up: bfloat16 [128, 2048, 512], P('req', None, 'tp'), may hold values from -0.125 to 0.125
- w_down: bfloat16 [128, 512, 2048], P('req', 'tp'), may hold values from -0.1875 to 0.1875
Outputs:
- layer_out: bfloat16 [512, 2048], P('req', 'tp')
Inputs may be any that keep to these rules, and one draw needn't show every extreme that they name: queries: the printed draw and the hidden one differ in row scales. `block_group`: exactly half of the 8 cache blocks belong to each group. `routes`: within the rows of one request, each expert is named by at most 10 rows, a bound that some block reaches. `lengths`: each request has at least one live suffix slot, and some request has all 64.
All inputs are finite; a program needn't handle non-finite values. No bound on the sum of `lengths` on one device may be relied on, other than what follows from the above.
Results may differ from a plain program's by a relative error of at most 0.025.
Values may be sent and summed in bfloat16 or wider, within the bound.
A program may use at most 128 MiB of HBM per device.

v0:
```python
import math
import jax
import jax.numpy as jnp
from jax import lax
from jax.sharding import PartitionSpec as P

HD = 128
E = 64
TOPK = 8
CAP = 10
epsilon = 1e-06


def slot_numbers(block_routes):
    flatten = block_routes.reshape(-1)
    chosen = (flatten[:, None] == jnp.arange(E, dtype=jnp.int32)[None, :]).astype(jnp.int32)
    earlier = jnp.cumsum(chosen, axis=0) - chosen
    return (flatten, jnp.sum(earlier * chosen, axis=1))


def body(
    hidden_in,
    queries,
    keys_new,
    values_new,
    prefix_keys,
    prefix_values,
    block_group,
    req_group,
    lengths,
    w_out,
    norm_gain,
    w_router,
    routes,
    w_gate,
    w_up,
    w_down,
):
    row_count = queries.shape[0]
    local_heads = queries.shape[1] // HD
    width = hidden_in.shape[1]
    factor = 1.0 / math.sqrt(HD)
    query_rows = queries.reshape(row_count, local_heads, HD)
    key_rows = keys_new.reshape(row_count, local_heads, HD)
    value_rows = values_new.reshape(row_count, local_heads, HD)
    group_id = req_group[0].astype(jnp.float32)
    own_valid = jnp.arange(row_count) < lengths[0]
    scores = (
        jnp.einsum("qhd,khd->hqk", query_rows, key_rows, preferred_element_type=jnp.float32)
        * factor
    )
    scores = jnp.where(own_valid[None, None, :], scores, -jnp.inf)
    top_score = jnp.max(scores, axis=-1)
    weights = jnp.exp(scores - top_score[..., None])
    best = top_score
    total = jnp.sum(weights, axis=-1)
    summed = jnp.einsum(
        "hqk,khd->hqd", weights.astype(jnp.bfloat16), value_rows, preferred_element_type=jnp.float32
    )
    piece_keys = lax.all_gather(prefix_keys, "req", axis=0, tiled=True)
    piece_values = lax.all_gather(prefix_values, "req", axis=0, tiled=True)
    piece_groups = lax.all_gather(block_group.astype(jnp.bfloat16), "req", axis=0, tiled=True)
    count = piece_keys.shape[0] * piece_keys.shape[1]
    flat_keys = piece_keys.reshape(count, local_heads, HD)
    flat_values = piece_values.reshape(count, local_heads, HD)
    key_valid = jnp.repeat(piece_groups.astype(jnp.float32), piece_keys.shape[1]) == group_id
    block_scores = (
        jnp.einsum("qhd,khd->hqk", query_rows, flat_keys, preferred_element_type=jnp.float32)
        * factor
    )
    block_scores = jnp.where(key_valid[None, None, :], block_scores, -jnp.inf)
    new_best = jnp.maximum(best, jnp.max(block_scores, axis=-1))
    shrink = jnp.exp(best - new_best)
    block_weights = jnp.exp(block_scores - new_best[..., None])
    added = jnp.einsum(
        "hqk,khd->hqd",
        block_weights.astype(jnp.bfloat16),
        flat_values,
        preferred_element_type=jnp.float32,
    )
    best, total, summed = (
        new_best,
        total * shrink + jnp.sum(block_weights, axis=-1),
        summed * shrink[..., None] + added,
    )
    mixed = (summed / total[..., None]).astype(jnp.bfloat16)
    mixed = jnp.transpose(mixed, (1, 0, 2)).reshape(row_count, local_heads * HD)
    partial_value = jnp.dot(mixed, w_out, preferred_element_type=jnp.float32)
    tp_count = lax.axis_size("tp")
    col_width = width // tp_count
    col_start = lax.axis_index("tp") * col_width
    whole = hidden_in.astype(jnp.float32) + lax.psum(
        partial_value.astype(jnp.bfloat16), "tp"
    ).astype(jnp.float32)
    mean_square = jnp.mean(whole * whole, axis=1, keepdims=True)
    normed = (
        whole * lax.rsqrt(mean_square + epsilon) * norm_gain.astype(jnp.float32)[None, :]
    ).astype(jnp.bfloat16)
    state_cols = lax.dynamic_slice_in_dim(whole, col_start, col_width, 1)
    logits = jnp.dot(normed.astype(jnp.float32), w_router, precision=lax.Precision.HIGHEST)
    expert_ids = jnp.arange(E, dtype=jnp.int32)
    picked = jnp.sum(
        jnp.where(routes[:, :, None] == expert_ids[None, None, :], logits[:, None, :], 0.0), axis=2
    )
    gates = jax.nn.softmax(picked, axis=1)
    flatten, slot = slot_numbers(routes)
    position = (flatten * CAP + slot).reshape(row_count, TOPK)
    columns = jnp.arange(E * CAP, dtype=jnp.int32)
    hits = position[:, :, None] == columns[None, None, :]
    placing = jnp.any(hits, axis=1).astype(jnp.bfloat16)
    outgoing = jnp.einsum("tc,td->cd", placing, normed, preferred_element_type=jnp.float32).astype(
        jnp.bfloat16
    )
    combining = jnp.sum(jnp.where(hits, gates[:, :, None], 0.0), axis=1)
    doubled = jnp.repeat(outgoing.reshape(E, CAP, width), 2, axis=0)
    received = lax.all_to_all(doubled, "req", split_axis=0, concat_axis=1, tiled=True)
    gate_val = jnp.einsum("lrd,ldf->lrf", received, w_gate, preferred_element_type=jnp.float32)
    up_val = jnp.einsum("lrd,ldf->lrf", received, w_up, preferred_element_type=jnp.float32)
    inner = (jax.nn.silu(gate_val) * up_val).astype(jnp.bfloat16)
    pieces = jnp.einsum("lrf,lfd->lrd", inner, w_down, preferred_element_type=jnp.float32).astype(
        jnp.bfloat16
    )
    returned = lax.all_to_all(pieces, "req", split_axis=1, concat_axis=0, tiled=True)
    summed_halves = jnp.sum(returned.reshape(E, 2, CAP, width).astype(jnp.float32), axis=1).reshape(
        E * CAP, width
    )
    expert_part = jnp.dot(
        combining,
        summed_halves,
        precision=lax.Precision.HIGHEST,
        preferred_element_type=jnp.float32,
    )
    expert_cols = lax.psum_scatter(
        expert_part.astype(jnp.bfloat16), "tp", scatter_dimension=1, tiled=True
    ).astype(jnp.float32)
    return (state_cols + expert_cols).astype(jnp.bfloat16)


def solution(mesh):
    in_specs = (
        P("req", None),
        P("req", "tp"),
        P("req", "tp"),
        P("req", "tp"),
        P("req", None, "tp"),
        P("req", None, "tp"),
        P("req"),
        P("req"),
        P("req"),
        P("tp", None),
        P(),
        P(),
        P("req", None),
        P("req", None, "tp"),
        P("req", None, "tp"),
        P("req", "tp", None),
    )
    out_specs = P("req", "tp")
    return jax.shard_map(body, mesh=mesh, in_specs=in_specs, out_specs=out_specs, check_vma=False)
```

profile of v0, /device:TPU:0, one launch (start us, length us, event | category | flops | bytes accessed | tf_op | source)
XLA Modules:
  0.0 582.9 jit_solution(14911283072433838208)
XLA Ops:
  8.7 1.2 dynamic-slice
  10.0 0.8 dynamic-update-slice
  10.7 23.1 %all-reduce = bf16[8]{0:T(256)(128)(2,1)S(1)} all-reduce(bf16[8]{0:T(256)(128)(2,1)S(1)} %dynamic-update-slice), channel_id=1, replica_groups=mesh['req'=8,'tp'=4] {'req'}, use_global_device_ids=true, to_apply=%add | all-reduce | flops 8 | bytes 32
  33.9 0.1 eq.67
  34.0 30.7 %all_gather.10 = bf16[8,16,512]{2,1,0:T(8,128)(2,1)S(1)} all-gather(bf16[1,16,512]{2,1,0:T(8,128)(2,1)} %param.20), channel_id=1, replica_groups=mesh['req'=8,'tp'=4] {'req'}, dimensions={0}, use_global_device_ids=true | all-gather | bytes 147456 | tf_op jit(solution)/shard_map/all_gather | solution.py:60
  64.8 30.7 %all_gather.11 = bf16[8,16,512]{2,1,0:T(8,128)(2,1)S(1)} all-gather(bf16[1,16,512]{2,1,0:T(8,128)(2,1)} %param.21), channel_id=1, replica_groups=mesh['req'=8,'tp'=4] {'req'}, dimensions={0}, use_global_device_ids=true | all-gather | bytes 147456 | tf_op jit(solution)/shard_map/all_gather | solution.py:61
  95.5 1.1 fusion.57
  96.7 1.1 fusion.56
  97.8 0.2 fusion.34
  98.0 1.1 fusion.14
  99.1 0.2 fusion.19
  99.3 1.2 convolution_convert_fusion.3
  100.5 0.1 copy.95
  100.6 0.1 eq.72
  100.7 0.1 eq.68
  100.8 1.2 reduce-window.6
  102.0 0.2 slice_reduce_fusion
  102.3 0.1 fusion.28
  102.4 0.1 reduce_sum.83
  102.6 0.1 copy.99
  102.7 0.5 fusion.4
  103.2 26.7 %all-reduce.3.cloned.1.call-done = bf16[64,2048]{1,0:T(8,128)(2,1)} async-done(((bf16[64,2048]{1,0:T(8,128)(2,1)}), bf16[64,2048]{1,0:T(8,128)(2,1)}) %all-reduce.3.cloned.1.call-update) | async-done | bytes 262160 | tf_op jit(solution)/shard_map/psum | solution.py:92
  129.9 1.1 convert_add_fusion
  131.0 3.4 convolution_convert_fusion.1
  134.4 5.4 reshape.145
  139.8 6.8 %broadcast_in_dim.79 = bf16[64,2,10,2048]{3,2,1,0:T(8,128)(2,1)} broadcast(bf16[64,10,2048]{2,1,0:T(8,128)(2,1)} %reshape.145), dimensions={0,2,3} | broadcast | bytes 7864320 | tf_op jit(solution)/shard_map/broadcast_in_dim | solution.py:115
  146.5 187.4 %all_to_all.27 = bf16[128,10,2048]{2,1,0:T(8,128)(2,1)S(1)} all-to-all(bf16[128,10,2048]{2,1,0:T(8,128)(2,1)} %bitcast.107), channel_id=1, replica_groups=mesh['req'=8,'tp'=4] {'req'}, dimensions={0} | all-to-all | bytes 10485760 | tf_op jit(solution)/shard_map/all_to_all | solution.py:116
  334.0 3.4 copy.105
  337.4 2.3 copy-done.2
  339.7 9.7 %fusion.2 = f32[16,80,128]{2,1,0:T(8,128)S(1)} fusion(bf16[16,2048,128]{2,1,0:T(8,128)(2,1)} %param.29, bf16[16,80,2048]{2,0,1:T(8,128)(2,1)S(1)} %bitcast.109), kind=kOutput, calls=%fused_computation.3 | convolution fusion | flops 671088640 | bytes 14286848 | tf_op jit(solution)/shard_map/lrd,ldf->lrf/dot_general | solution.py:117
  349.5 17.3 %convolution_convert_fusion = bf16[16,80,2048]{2,1,0:T(8,128)(2,1)} fusion(bf16[16,128,2048]{2,1,0:T(8,128)(2,1)} %param.31, bf16[16,2048,128]{2,1,0:T(8,128)(2,1)} %param.30, bf16[16,80,2048]{2,0,1:T(8,128)(2,1)} %bitcast.110, f32[16,80,128]{2,1,0:T(8,128)S(1)} %fusion.2), kind=kOutput, calls=%fused_computation.5 | convolution fusion | flops 1345781760 | bytes 27918336 | tf_op jit(solution)/shard_map/lrf,lfd->lrd/dot_general | solution.py:120
  366.8 7.7 %copy.108 = bf16[16,80,2048]{2,0,1:T(8,128)(2,1)} copy(bf16[16,80,2048]{2,1,0:T(8,128)(2,1)} %convolution_convert_fusion) | data formatting | bytes 10485760 | tf_op jit(solution)/shard_map/convert_element_type | solution.py:120
  374.5 4.8 all-to-all-start.1
  379.3 0.5 fusion.54
  379.8 0.2 select_reduce_fusion.1
  380.1 0.1 reduce_max.35
  380.2 0.1 copy.103
  380.3 0.5 select_reduce_fusion
  380.8 113.0 %all-to-all-done.1 = bf16[16,80,2048]{2,0,1:T(8,128)(2,1)} async-done(((bf16[16,80,2048]{2,0,1:T(8,128)(2,1)}), bf16[16,80,2048]{2,0,1:T(8,128)(2,1)}, u32[]{:S(2)}, u32[]{:S(2)}) %all-to-all-start.1) | async-done | bytes 5242912 | tf_op jit(solution)/shard_map/all_to_all | solution.py:123
  493.8 3.9 convert_bitcast_fusion
  497.7 4.7 copy.109
  502.4 13.1 %reshape.148 = f32[64,2,10,2048]{3,1,0,2:T(2,128)} reshape(f32[8,16,10,2048]{3,1,0,2:T(8,128)} %copy.109) | data formatting | bytes 20971520 | tf_op jit(solution)/shard_map/convert_element_type | solution.py:124
  515.5 17.0 %reduce_sum.88 = f32[64,10,2048]{2,0,1:T(8,128)} reduce(f32[64,2,10,2048]{3,1,0,2:T(2,128)} %reshape.148, f32[]{:T(128)} %constant.14.clone.1), dimensions={1}, to_apply=%region_14.15 | reduce | flops 1310720 | bytes 15728644 | tf_op jit(solution)/shard_map/reduce_sum | solution.py:124
  532.5 8.9 %copy.110 = f32[64,10,2048]{2,1,0:T(8,128)} copy(f32[64,10,2048]{2,0,1:T(8,128)} %reduce_sum.88) | data formatting | bytes 10485760 | tf_op jit(solution)/shard_map/reduce_sum | solution.py:124
  541.4 7.6 %reshape.147 = f32[640,2048]{1,0:T(8,128)} reshape(f32[64,10,2048]{2,1,0:T(8,128)} %copy.110) | data formatting | bytes 10485760 | tf_op jit(solution)/shard_map/reshape | solution.py:124
  549.0 6.4 %convolution_convert_fusion.2 = bf16[64,2048]{1,0:T(8,128)(2,1)} fusion(f32[64,640]{1,0:T(8,128)S(1)} %select_reduce_fusion, f32[640,2048]{1,0:T(8,128)} %reshape.147), kind=kOutput, calls=%fused_computation.7 | convolution fusion | flops 1006764032 | bytes 5668864 | tf_op jit(solution)/shard_map/dot_general | solution.py:127
  555.4 18.9 %reduce-scatter.2.cloned.1.call-done = bf16[64,512]{1,0:T(8,128)(2,1)} async-done(((bf16[64,2048]{1,0:T(8,128)(2,1)}), bf16[64,512]{1,0:T(8,128)(2,1)}) %reduce-scatter.2.cloned.1.call-update) | async-done | bytes 65552 | tf_op jit(solution)/shard_map/reduce_scatter | solution.py:133
  574.3 1.5 add_convert_fusion
  (38 shorter events, 0.6 us)
Async XLA Ops:
  6.5 92.8 %copy-start = (bf16[512,2048]{1,0:T(8,128)(2,1)S(1)}, bf16[512,2048]{1,0:T(8,128)(2,1)}, u32[]{:S(2)}) copy-start(bf16[512,2048]{1,0:T(8,128)(2,1)} %param.25) | copy-start | bytes 6291460
  6.5 94.0 %copy-start.6 = (s32[64,8]{0,1:T(8,128)S(1)}, s32[64,8]{0,1:T(8,128)}, u32[]{:S(2)}) copy-start(s32[64,8]{0,1:T(8,128)} %param.28) | copy-start | bytes 6148
  6.5 94.2 %copy-start.7 = (bf16[2048]{0:T(1024)(128)(2,1)S(1)}, bf16[2048]{0:T(1024)(128)(2,1)}, u32[]{:S(2)}) copy-start(bf16[2048]{0:T(1024)(128)(2,1)} %param.26) | copy-start | bytes 12292
  6.5 123.3 %copy-start.3 = (bf16[64,2048]{1,0:T(8,128)(2,1)S(1)}, bf16[64,2048]{1,0:T(8,128)(2,1)}, u32[]{:S(2)}) copy-start(bf16[64,2048]{1,0:T(8,128)(2,1)} %param.16) | copy-start | bytes 786436
  6.5 123.3 %all-reduce.3.cloned.1.call-start = ((), (), s32[]{:S(2)}) async-start(), calls=%async_computation.3 | async-start | bytes 524288 | tf_op jit(solution)/shard_map/psum | solution.py:92
  337.4 2.3 copy-start.2
  374.4 4.9 copy-start.4
  374.5 4.9 copy-start.5
  374.5 119.4 %all-to-all-start.1 = ((bf16[16,80,2048]{2,0,1:T(8,128)(2,1)}), bf16[16,80,2048]{2,0,1:T(8,128)(2,1)}, u32[]{:S(2)}, u32[]{:S(2)}) async-start(bf16[16,80,2048]{2,0,1:T(8,128)(2,1)} %copy.108), calls=%async_computation.1 | async-start | bytes 10485760 | tf_op jit(solution)/shard_map/all_to_all | solution.py:123
  379.3 195.1 %reduce-scatter.2.cloned.1.call-start = ((), (), s32[]{:S(2)}) async-start(), calls=%async_computation.4 | async-start | bytes 327680 | tf_op jit(solution)/shard_map/reduce_scatter | solution.py:133
  541.4 34.4 %copy-start.1 = (bf16[512,2048]{1,0:T(8,128)(2,1)S(1)}, bf16[512,2048]{1,0:T(8,128)(2,1)}, u32[]{:S(2)}) copy-start(bf16[512,2048]{1,0:T(8,128)(2,1)} %param.25) | copy-start | bytes 6291460
Sparse Core Ops, SparseCore 0:
  100.6 29.2 all-reduce.2
  555.6 18.7 reduce-scatter.1
where the time goes:
time: 588 us; the launch traced here: 583 us
  blocking collectives  272 us (46%)
  waiting for transfers between devices  159 us (27%)
  local copies, waits for them, and re-layouts  63 us (11%)
  matrix products  41.9 us (7%)
  other arithmetic  26.5 us (5%)
  between operations  16 us (3%)
    all_to_all x1, blocking collectives, body(): lax.all_to_all(doubled, 'req', split_axis=0, concat_axis=1, tiled=True)  187 us
    all_to_all x1, waiting for transfers between devices, body(): lax.all_to_all(pieces, 'req', split_axis=1, concat_axis=0, tiled=True)  113 us
    all_gather x1, blocking collectives, body(): piece_values = lax.all_gather(prefix_values, 'req', axis=0, tiled=True)  30.7 us
    all_gather x1, blocking collectives, body(): piece_keys = lax.all_gather(prefix_keys, 'req', axis=0, tiled=True)  30.7 us
    psum x1, waiting for transfers between devices, body(): lax.psum(partial_value.astype(jnp.bfloat16), 'tp').astype(jnp.float32)  26.7 us
    unnamed x1, blocking collectives  23.1 us
    reduce_scatter x1, waiting for transfers between devices, body(): lax.psum_scatter(expert_part.astype(jnp.bfloat16), 'tp', scatter_dimensio...  18.9 us
    convert_element_type x2, local copies, waits for them, and re-layouts, body(): returned.reshape(E, 2, CAP, width).astype(jnp.float32)  17.8 us
  transfers between devices with their start and end apart: 3, of which 3 were waited for; matrix products, arithmetic and copies ran while one was open for 1% of the time, Pallas kernels for 0%

commit v1 on v0

--- a/solution.py
+++ b/solution.py
@@ -120,7 +120,10 @@
     pieces = jnp.einsum("lrf,lfd->lrd", inner, w_down, preferred_element_type=jnp.float32).astype(
         jnp.bfloat16
     )
-    returned = lax.all_to_all(pieces, "req", split_axis=1, concat_axis=0, tiled=True)
+    returned = jnp.concatenate(
+        lax.all_to_all(jnp.stack(jnp.split(pieces, lax.axis_size("req"), axis=1)), "req", 0, 0),
+        axis=0,
+    )
     summed_halves = jnp.sum(returned.reshape(E, 2, CAP, width).astype(jnp.float32), axis=1).reshape(
         E * CAP, width
     )

time: 588 us -> 594 us (1.010)
  local copies, waits for them, and re-layouts: 63 us -> 72.8 us
    unnamed x20 -> x25, local copies, waits for them, and re-layouts: 4.42 us -> 13.3 us
    convert_element_type x1 -> x0, local copies, waits for them, and re-layouts: 7.67 us -> none  [body(): jnp.einsum('lrf,lfd->lrd', inner, w_down, preferred_element_type=jnp.floa...]
where the time goes in v1:
time: 594 us; the launch traced here: 588 us
  blocking collectives  272 us (46%)
  waiting for transfers between devices  156 us (26%)
  local copies, waits for them, and re-layouts  72.8 us (12%)
  matrix products  42 us (7%)
  other arithmetic  24 us (4%)
  between operations  16 us (3%)
    all_to_all x1, blocking collectives, body(): lax.all_to_all(doubled, 'req', split_axis=0, concat_axis=1, tiled=True)  187 us
    all_to_all x1, waiting for transfers between devices, body(): lax.all_to_all(jnp.stack(jnp.split(pieces, lax.axis_size('req'), axis=1))...  113 us
    all_gather x1, blocking collectives, body(): piece_values = lax.all_gather(prefix_values, 'req', axis=0, tiled=True)  30.7 us
    all_gather x1, blocking collectives, body(): piece_keys = lax.all_gather(prefix_keys, 'req', axis=0, tiled=True)  30.7 us
    psum x1, waiting for transfers between devices, body(): lax.psum(partial_value.astype(jnp.bfloat16), 'tp').astype(jnp.float32)  24.7 us
    unnamed x1, blocking collectives  23.1 us
    convert_element_type x2, local copies, waits for them, and re-layouts, body(): returned.reshape(E, 2, CAP, width).astype(jnp.float32)  20.8 us
    reduce_scatter x1, waiting for transfers between devices, body(): lax.psum_scatter(expert_part.astype(jnp.bfloat16), 'tp', scatter_dimensio...  18.8 us
  transfers between devices with their start and end apart: 3, of which 3 were waited for; matrix products, arithmetic and copies ran while one was open for 1% of the time, Pallas kernels for 0%

profile of v1, /device:TPU:0, one launch (start us, length us, event | category | flops | bytes accessed | tf_op | source)
XLA Modules:
  0.0 588.3 jit_solution(4179388420171971236)
XLA Ops:
  8.7 1.2 dynamic-slice
  9.9 0.8 dynamic-update-slice
  10.7 23.1 %all-reduce = bf16[8]{0:T(256)(128)(2,1)S(1)} all-reduce(bf16[8]{0:T(256)(128)(2,1)S(1)} %dynamic-update-slice), channel_id=1, replica_groups=mesh['req'=8,'tp'=4] {'req'}, use_global_device_ids=true, to_apply=%add | all-reduce | flops 8 | bytes 32
  34.0 30.7 %all_gather.10 = bf16[8,16,512]{2,1,0:T(8,128)(2,1)S(1)} all-gather(bf16[1,16,512]{2,1,0:T(8,128)(2,1)} %param.20), channel_id=1, replica_groups=mesh['req'=8,'tp'=4] {'req'}, dimensions={0}, use_global_device_ids=true | all-gather | bytes 147456 | tf_op jit(solution)/shard_map/all_gather | solution.py:60
  64.7 30.7 %all_gather.11 = bf16[8,16,512]{2,1,0:T(8,128)(2,1)S(1)} all-gather(bf16[1,16,512]{2,1,0:T(8,128)(2,1)} %param.21), channel_id=1, replica_groups=mesh['req'=8,'tp'=4] {'req'}, dimensions={0}, use_global_device_ids=true | all-gather | bytes 147456 | tf_op jit(solution)/shard_map/all_gather | solution.py:61
  95.5 1.1 fusion.65
  96.6 1.0 fusion.64
  97.9 1.1 fusion.14
  99.0 0.2 fusion.19
  99.3 1.2 convolution_convert_fusion.3
  100.5 0.8 copy.132
  101.4 0.7 convert_element_type.82
  102.1 1.2 reduce-window.6
  103.3 0.2 slice_reduce_fusion
  103.9 0.7 multiply_add_fusion
  104.7 0.5 fusion.4
  105.1 24.7 %all-reduce.3.cloned.1.call-done = bf16[64,2048]{1,0:T(8,128)(2,1)} async-done(((bf16[64,2048]{1,0:T(8,128)(2,1)}), bf16[64,2048]{1,0:T(8,128)(2,1)}) %all-reduce.3.cloned.1.call-update) | async-done | bytes 262160 | tf_op jit(solution)/shard_map/psum | solution.py:92
  129.8 1.2 convert_add_fusion
  131.1 3.5 convolution_convert_fusion.1
  134.5 5.4 reshape.141
  139.9 6.8 %broadcast_in_dim.79 = bf16[64,2,10,2048]{3,2,1,0:T(8,128)(2,1)} broadcast(bf16[64,10,2048]{2,1,0:T(8,128)(2,1)} %reshape.141), dimensions={0,2,3} | broadcast | bytes 7864320 | tf_op jit(solution)/shard_map/broadcast_in_dim | solution.py:115
  146.7 187.4 %all_to_all.23 = bf16[128,10,2048]{2,1,0:T(8,128)(2,1)S(1)} all-to-all(bf16[128,10,2048]{2,1,0:T(8,128)(2,1)} %bitcast.135), channel_id=1, replica_groups=mesh['req'=8,'tp'=4] {'req'}, dimensions={0} | all-to-all | bytes 10485760 | tf_op jit(solution)/shard_map/all_to_all | solution.py:116
  334.1 3.4 copy.142
  337.5 2.3 copy-done.3
  339.8 9.7 %fusion.2 = f32[16,80,128]{2,1,0:T(8,128)S(1)} fusion(bf16[16,2048,128]{2,1,0:T(8,128)(2,1)} %param.29, bf16[16,80,2048]{2,0,1:T(8,128)(2,1)S(1)} %bitcast.137), kind=kOutput, calls=%fused_computation.2 | convolution fusion | flops 671088640 | bytes 14286848 | tf_op jit(solution)/shard_map/lrd,ldf->lrf/dot_general | solution.py:117
  349.6 17.3 %convolution_convert_fusion = bf16[16,80,2048]{2,1,0:T(8,128)(2,1)} fusion(bf16[16,128,2048]{2,1,0:T(8,128)(2,1)} %param.31, bf16[16,2048,128]{2,1,0:T(8,128)(2,1)} %param.30, bf16[16,80,2048]{2,0,1:T(8,128)(2,1)} %bitcast.138, f32[16,80,128]{2,1,0:T(8,128)S(1)} %fusion.2), kind=kOutput, calls=%fused_computation.4 | convolution fusion | flops 1345781760 | bytes 27918336 | tf_op jit(solution)/shard_map/lrf,lfd->lrd/dot_general | solution.py:120
  366.9 1.4 fusion.27
  368.3 2.2 fusion.26
  370.5 1.8 fusion.25
  372.4 1.8 fusion.24
  374.3 0.4 fusion.22
  374.7 0.4 fusion.21
  375.2 0.3 fusion.20
  375.4 5.3 copy.145
  380.8 4.8 all-to-all-start.1
  385.6 0.3 reduce-scatter.2.cloned.1.call-start
  385.9 0.5 fusion.62
  386.4 0.2 select_reduce_fusion.1
  386.9 0.5 select_reduce_fusion
  387.4 112.8 %all-to-all-done.1 = bf16[8,16,10,2048]{3,1,2,0:T(8,128)(2,1)} async-done(((bf16[8,16,10,2048]{3,1,2,0:T(8,128)(2,1)}), bf16[8,16,10,2048]{3,1,2,0:T(8,128)(2,1)}, u32[]{:S(2)}, u32[]{:S(2)}) %all-to-all-start.1) | async-done | bytes 5242912 | tf_op jit(solution)/shard_map/all_to_all | solution.py:124
  500.2 7.9 %copy.146 = f32[8,16,10,2048]{3,1,0,2:T(8,128)} copy(bf16[8,16,10,2048]{3,1,2,0:T(8,128)(2,1)} %all-to-all-done.1) | data formatting | bytes 15728640 | tf_op jit(solution)/shard_map/convert_element_type | solution.py:127
  508.1 12.9 %reshape.144 = f32[64,2,10,2048]{3,1,0,2:T(2,128)} reshape(f32[8,16,10,2048]{3,1,0,2:T(8,128)} %copy.146) | data formatting | bytes 20971520 | tf_op jit(solution)/shard_map/convert_element_type | solution.py:127
  521.0 16.9 %reduce_sum.88 = f32[64,10,2048]{2,0,1:T(8,128)} reduce(f32[64,2,10,2048]{3,1,0,2:T(2,128)} %reshape.144, f32[]{:T(128)} %constant.14.clone.1), dimensions={1}, to_apply=%region_14.15 | reduce | flops 1310720 | bytes 15728644 | tf_op jit(solution)/shard_map/reduce_sum | solution.py:127
  538.0 9.1 %copy.147 = f32[64,10,2048]{2,1,0:T(8,128)} copy(f32[64,10,2048]{2,0,1:T(8,128)} %reduce_sum.88) | data formatting | bytes 10485760 | tf_op jit(solution)/shard_map/reduce_sum | solution.py:127
  547.1 7.4 %reshape.143 = f32[640,2048]{1,0:T(8,128)} reshape(f32[64,10,2048]{2,1,0:T(8,128)} %copy.147) | data formatting | bytes 10485760 | tf_op jit(solution)/shard_map/reshape | solution.py:127
  554.5 6.4 %convolution_convert_fusion.2 = bf16[64,2048]{1,0:T(8,128)(2,1)} fusion(f32[64,640]{1,0:T(8,128)S(1)} %select_reduce_fusion, f32[640,2048]{1,0:T(8,128)} %reshape.143), kind=kOutput, calls=%fused_computation.6 | convolution fusion | flops 1006764032 | bytes 5668864 | tf_op jit(solution)/shard_map/dot_general | solution.py:130
  560.9 18.8 %reduce-scatter.2.cloned.1.call-done = bf16[64,512]{1,0:T(8,128)(2,1)} async-done(((bf16[64,2048]{1,0:T(8,128)(2,1)}), bf16[64,512]{1,0:T(8,128)(2,1)}) %reduce-scatter.2.cloned.1.call-update) | async-done | bytes 65552 | tf_op jit(solution)/shard_map/reduce_scatter | solution.py:136
  579.8 1.5 add_convert_fusion
  (43 shorter events, 1.5 us)
Async XLA Ops:
  6.5 92.7 %copy-start = (bf16[512,2048]{1,0:T(8,128)(2,1)S(1)}, bf16[512,2048]{1,0:T(8,128)(2,1)}, u32[]{:S(2)}) copy-start(bf16[512,2048]{1,0:T(8,128)(2,1)} %param.25) | copy-start | bytes 6291460
  6.5 123.3 %all-reduce.3.cloned.1.call-start = ((), (), s32[]{:S(2)}) async-start(), calls=%async_computation.3 | async-start | bytes 524288 | tf_op jit(solution)/shard_map/psum | solution.py:92
  337.5 2.3 copy-start.3
  366.9 7.3 %copy-start.2 = (bf16[16,80,2048]{2,1,0:T(8,128)(2,1)S(1)}, bf16[16,80,2048]{2,1,0:T(8,128)(2,1)}, u32[]{:S(2)}) copy-start(bf16[16,80,2048]{2,1,0:T(8,128)(2,1)} %convolution_convert_fusion) | copy-start | bytes 15728644
  380.8 5.1 copy-start.4
  380.8 5.1 copy-start.5
  380.8 5.1 copy-start.6
  380.8 119.4 %all-to-all-start.1 = ((bf16[8,16,10,2048]{3,1,2,0:T(8,128)(2,1)}), bf16[8,16,10,2048]{3,1,2,0:T(8,128)(2,1)}, u32[]{:S(2)}, u32[]{:S(2)}) async-start(bf16[8,16,10,2048]{3,1,2,0:T(8,128)(2,1)} %copy.145), calls=%async_computation.1 | async-start | bytes 10485760 | tf_op jit(solution)/shard_map/all_to_all | solution.py:124
  385.6 194.1 %reduce-scatter.2.cloned.1.call-start = ((), (), s32[]{:S(2)}) async-start(), calls=%async_computation.4 | async-start | bytes 327680 | tf_op jit(solution)/shard_map/reduce_scatter | solution.py:136
  538.0 43.3 %copy-start.1 = (bf16[512,2048]{1,0:T(8,128)(2,1)S(1)}, bf16[512,2048]{1,0:T(8,128)(2,1)}, u32[]{:S(2)}) copy-start(bf16[512,2048]{1,0:T(8,128)(2,1)} %param.25) | copy-start | bytes 6291460
Sparse Core Ops, SparseCore 0:
  100.6 29.2 all-reduce.2
  561.0 18.6 reduce-scatter.1
